TPU v7x, 512 devices: a whole 4x8x8 slice. The times are simulated.
512 devices in a mesh: tm: 16 (over y_lo, z), space: 32 (over x, y_hi, core).
Axes of the slice: x: 4, y: 8 (y_hi: 4, y_lo: 2; y = y_hi * 2 + y_lo), z: 8, core: 2. Of those that a mesh axis runs over, the one named last changes fastest.
Arguments:
- region_map: int32 [256, 128, 128], P('space'), may hold values from 0 to 7
- region_coef: float32 [8], replicated, may hold values from 0.08 to 0.32
- source_cell: int32 [32768], P('space'), may hold values from 0 to 131071
- amplitude: float32 [16, 8, 32768], P('tm', None, 'space'), may hold values from -4 to 4
Outputs:
- states: float32 [16, 2, 256, 128, 128], P('tm', None, 'space')
All inputs are finite; a program needn't handle non-finite values.
Results may differ from a plain program's by a relative error of at most 0.00002.
Values sent between devices are 32-bit elements; how exact they have to be, the bound alone decides.
A program may use at most 64 MiB of HBM per device.

v0:
```python
import jax
import jax.numpy as jnp
from jax import lax
from jax.sharding import PartitionSpec as P

STEPS = 8
SPAN = 3


def extended(cells, sides, width):
    for axis, dim in sides:
        count = lax.axis_size(axis)
        ends = count - 1
        head = lax.slice_in_dim(cells, 0, width, axis=dim)
        tail = lax.slice_in_dim(cells, cells.shape[dim] - width, cells.shape[dim], axis=dim)
        cells = jnp.concatenate(
            [
                lax.ppermute(tail, axis, [(i, (i + 1) % count) for i in range(ends)]),
                cells,
                lax.ppermute(head, axis, [((i + 1) % count, i) for i in range(ends)]),
            ],
            axis=dim,
        )
    return cells


def passed_along(block, axis, distance):
    devices = range(lax.axis_size(axis))
    route = [(i - distance, i) for i in devices if i - distance in devices]
    return lax.ppermute(block, axis, route)


def shards(region_map, region_coef, source_cell, amplitude):
    courant = jnp.zeros(region_map.shape, jnp.float32)
    for region in range(region_coef.shape[0]):
        courant = courant + jnp.where(region_map == region, region_coef[region], 0.0)
    zero_field = jnp.zeros(region_map.shape, jnp.float32)
    planes_dev = region_map.shape[0]
    slab_cells = planes_dev * region_map.shape[1] * region_map.shape[2]

    def make_forcing(wavelet_row):
        return (
            jnp.zeros((slab_cells,), jnp.float32)
            .at[source_cell]
            .add(wavelet_row)
            .reshape(region_map.shape)
        )

    def laplace(field):
        padded = extended(field, (("space", 0),), 1)
        padded = jnp.pad(padded, ((0, 0), (1, 1), (1, 1)))
        beside = padded[2:, 1:-1, 1:-1] + padded[:-2, 1:-1, 1:-1]
        beside = beside + padded[1:-1, 2:, 1:-1] + padded[1:-1, :-2, 1:-1]
        beside = beside + padded[1:-1, 1:-1, 2:] + padded[1:-1, 1:-1, :-2]
        return beside - 6.0 * field

    def leap_step(carried_pair, forcing):
        earlier, current = carried_pair
        newest = 2.0 * current - earlier + courant * laplace(current) + forcing
        return (current, newest)

    own_wavelets = amplitude[0]

    def forced_advance(which_step, carried_pair):
        return leap_step(carried_pair, make_forcing(own_wavelets[which_step]))

    own_pair = lax.fori_loop(0, STEPS, forced_advance, (zero_field, zero_field))
    summed = own_pair
    moving = own_pair
    for hops in range(1, SPAN + 1):

        def homogeneous_advance(which_step, carried_pair):
            return leap_step(carried_pair, zero_field)

        moving = lax.fori_loop(0, STEPS, homogeneous_advance, moving)
        arrived = passed_along(jnp.stack([moving[0], moving[1]]), "tm", hops)
        summed = (summed[0] + arrived[0], summed[1] + arrived[1])
    return jnp.stack([summed[0], summed[1]])[None]


def solution(mesh):
    placed = (P("space", None, None), P(), P("space"), P("tm", None, "space"))
    return jax.shard_map(
        shards,
        mesh=mesh,
        in_specs=placed,
        out_specs=P("tm", None, "space", None, None),
        check_vma=False,
    )
```

profile of v0, /device:TPU:454, one launch (start us, length us, event | category | flops | bytes accessed | tf_op | source)
XLA Modules:
  0.0 533.8 jit_solution(5215837111816725763)
XLA Ops:
  1.6 6.4 %select_add_fusion = f32[8,128,128]{2,1,0:T(8,128)S(1)} fusion(s32[8,128,128]{2,1,0:T(8,128)} %param.12, f32[]{:T(128)} %bitcast.7, f32[]{:T(128)} %bitcast.6, f32[]{:T(128)} %bitcast.5, f32[]{:T(128)} %bitcast.4, f32[]{:T(128)} %bitcast.3, f32[]{:T(128)} %bitcast.2, f32[]{:T(128)} %bitcast.1, f32[]{:T(128)} %bitcast), kind=kLoop, calls=%fused_computation.101 | loop fusion | flops 3014656 | bytes 1048608 | tf_op jit(solution)/shard_map/add | solution.py:36
  8.1 132.0 %while.63 = (s32[]{:T(128)}, f32[8,128,128]{2,1,0:T(8,128)S(1)}, f32[8,128,128]{2,1,0:T(8,128)S(1)}, f32[8,128,128]{2,1,0:T(8,128)S(1)}, s32[1024]{0:T(1024)S(1)...) while((s32[]{:T(128)}, f32[8,128,128]{2,1,0:T(8,128)S(1)}, ...), condition=%wide.region_2.3_spmd.clone, body=%wide.region_0.2_spmd.clone.sunk | while | flops 4505179 | bytes 9605479 | solution.py:67
  24.0 6.7 %collective-permute-start.6 = (f32[1,128,128]{2,1,0:T(8,128)S(1)}, f32[1,128,128]{2,1,0:T(8,128)S(1)}, u32[]{:S(2)}, u32[]{:S(2)}) collective-permute-start(f32[1,128,128]{2,1,0:T(8,128)S(1)} %get-tuple-element.531), channel_id=1, source_target_pairs={{1,0},{2,1},{3,2},{4,3},{5,4},{6,5},{7,6},{8,7},{9,8},{10,9},{11,1... | collective-permute-start | bytes 196616 | tf_op jit(solution)/shard_map/while/body/eval_jaxpr/ppermute | solution.py:20
  40.6 6.7 %collective-permute-start.6 = (f32[1,128,128]{2,1,0:T(8,128)S(1)}, f32[1,128,128]{2,1,0:T(8,128)S(1)}, u32[]{:S(2)}, u32[]{:S(2)}) collective-permute-start(f32[1,128,128]{2,1,0:T(8,128)S(1)} %get-tuple-element.531), channel_id=1, source_target_pairs={{1,0},{2,1},{3,2},{4,3},{5,4},{6,5},{7,6},{8,7},{9,8},{10,9},{11,1... | collective-permute-start | bytes 196616 | tf_op jit(solution)/shard_map/while/body/eval_jaxpr/ppermute | solution.py:20
  57.2 6.7 %collective-permute-start.6 = (f32[1,128,128]{2,1,0:T(8,128)S(1)}, f32[1,128,128]{2,1,0:T(8,128)S(1)}, u32[]{:S(2)}, u32[]{:S(2)}) collective-permute-start(f32[1,128,128]{2,1,0:T(8,128)S(1)} %get-tuple-element.531), channel_id=1, source_target_pairs={{1,0},{2,1},{3,2},{4,3},{5,4},{6,5},{7,6},{8,7},{9,8},{10,9},{11,1... | collective-permute-start | bytes 196616 | tf_op jit(solution)/shard_map/while/body/eval_jaxpr/ppermute | solution.py:20
  73.8 6.7 %collective-permute-start.6 = (f32[1,128,128]{2,1,0:T(8,128)S(1)}, f32[1,128,128]{2,1,0:T(8,128)S(1)}, u32[]{:S(2)}, u32[]{:S(2)}) collective-permute-start(f32[1,128,128]{2,1,0:T(8,128)S(1)} %get-tuple-element.531), channel_id=1, source_target_pairs={{1,0},{2,1},{3,2},{4,3},{5,4},{6,5},{7,6},{8,7},{9,8},{10,9},{11,1... | collective-permute-start | bytes 196616 | tf_op jit(solution)/shard_map/while/body/eval_jaxpr/ppermute | solution.py:20
  90.4 6.7 %collective-permute-start.6 = (f32[1,128,128]{2,1,0:T(8,128)S(1)}, f32[1,128,128]{2,1,0:T(8,128)S(1)}, u32[]{:S(2)}, u32[]{:S(2)}) collective-permute-start(f32[1,128,128]{2,1,0:T(8,128)S(1)} %get-tuple-element.531), channel_id=1, source_target_pairs={{1,0},{2,1},{3,2},{4,3},{5,4},{6,5},{7,6},{8,7},{9,8},{10,9},{11,1... | collective-permute-start | bytes 196616 | tf_op jit(solution)/shard_map/while/body/eval_jaxpr/ppermute | solution.py:20
  107.0 6.7 %collective-permute-start.6 = (f32[1,128,128]{2,1,0:T(8,128)S(1)}, f32[1,128,128]{2,1,0:T(8,128)S(1)}, u32[]{:S(2)}, u32[]{:S(2)}) collective-permute-start(f32[1,128,128]{2,1,0:T(8,128)S(1)} %get-tuple-element.531), channel_id=1, source_target_pairs={{1,0},{2,1},{3,2},{4,3},{5,4},{6,5},{7,6},{8,7},{9,8},{10,9},{11,1... | collective-permute-start | bytes 196616 | tf_op jit(solution)/shard_map/while/body/eval_jaxpr/ppermute | solution.py:20
  123.6 6.7 %collective-permute-start.6 = (f32[1,128,128]{2,1,0:T(8,128)S(1)}, f32[1,128,128]{2,1,0:T(8,128)S(1)}, u32[]{:S(2)}, u32[]{:S(2)}) collective-permute-start(f32[1,128,128]{2,1,0:T(8,128)S(1)} %get-tuple-element.531), channel_id=1, source_target_pairs={{1,0},{2,1},{3,2},{4,3},{5,4},{6,5},{7,6},{8,7},{9,8},{10,9},{11,1... | collective-permute-start | bytes 196616 | tf_op jit(solution)/shard_map/while/body/eval_jaxpr/ppermute | solution.py:20
  140.2 97.9 %while.60 = (s32[]{:T(128)}, f32[8,128,128]{2,1,0:T(8,128)S(1)}, f32[8,128,128]{2,1,0:T(8,128)S(1)}, f32[8,128,128]{2,1,0:T(8,128)S(1)}, s32[]{:T(128)}) while((s32[]{:T(128)}, f32[8,128,128]{2,1,0:T(8,128)S(1)}, f32[8,128,128]{2,1,0:T(8,128)S(1)}, f32[8,128,128]{2,1,0:T(8,128)S(1)}, s32[]{:T(128)}) %tuple.135), condition=%wide.region_4.5_spmd, body=%wide.region_3.4_spmd.sunk | while | flops 4238938 | bytes 8540461 | solution.py:75
  140.2 6.7 %collective-permute-start = (f32[1,128,128]{2,1,0:T(8,128)S(1)}, f32[1,128,128]{2,1,0:T(8,128)S(1)}, u32[]{:S(2)}, u32[]{:S(2)}) collective-permute-start(f32[1,128,128]{2,1,0:T(8,128)S(1)} %get-tuple-element.511), channel_id=1, source_target_pairs={{1,0},{2,1},{3,2},{4,3},{5,4},{6,5},{7,6},{8,7},{9,8},{10,9},{11,1... | collective-permute-start | bytes 196616 | tf_op jit(solution)/shard_map/while/body/eval_jaxpr/ppermute | solution.py:20
  230.7 6.3 %collective-permute-done.1 = f32[1,128,128]{2,1,0:T(8,128)S(1)} collective-permute-done((f32[1,128,128]{2,1,0:T(8,128)S(1)}, f32[1,128,128]{2,1,0:T(8,128)S(1)}, u32[]{:S(2)}, u32[]{:S(2)}) %collective-permute-start.1) | collective-permute-done | bytes 65568 | tf_op jit(solution)/shard_map/while/body/eval_jaxpr/ppermute | solution.py:18
  241.1 103.0 %while.61 = (s32[]{:T(128)}, f32[8,128,128]{2,1,0:T(8,128)S(1)}, f32[8,128,128]{2,1,0:T(8,128)S(1)}, f32[8,128,128]{2,1,0:T(8,128)S(1)}, s32[]{:T(128)}) while((s32[]{:T(128)}, f32[8,128,128]{2,1,0:T(8,128)S(1)}, f32[8,128,128]{2,1,0:T(8,128)S(1)}, f32[8,128,128]{2,1,0:T(8,128)S(1)}, s32[]{:T(128)}) %tuple.136), condition=%wide.region_6.7_spmd, body=%wide.region_5.6_spmd.sunk | while | flops 4238938 | bytes 8540461 | solution.py:75
  245.4 15.9 %collective-permute-done.3 = f32[1,128,128]{2,1,0:T(8,128)S(1)} collective-permute-done((f32[1,128,128]{2,1,0:T(8,128)S(1)}, f32[1,128,128]{2,1,0:T(8,128)S(1)}, u32[]{:S(2)}, u32[]{:S(2)}) %collective-permute-start.3) | collective-permute-done | bytes 65568 | tf_op jit(solution)/shard_map/while/body/eval_jaxpr/ppermute | solution.py:18
  266.8 6.2 %collective-permute-done.3 = f32[1,128,128]{2,1,0:T(8,128)S(1)} collective-permute-done((f32[1,128,128]{2,1,0:T(8,128)S(1)}, f32[1,128,128]{2,1,0:T(8,128)S(1)}, u32[]{:S(2)}, u32[]{:S(2)}) %collective-permute-start.3) | collective-permute-done | bytes 65568 | tf_op jit(solution)/shard_map/while/body/eval_jaxpr/ppermute | solution.py:18
  278.5 6.2 %collective-permute-done.3 = f32[1,128,128]{2,1,0:T(8,128)S(1)} collective-permute-done((f32[1,128,128]{2,1,0:T(8,128)S(1)}, f32[1,128,128]{2,1,0:T(8,128)S(1)}, u32[]{:S(2)}, u32[]{:S(2)}) %collective-permute-start.3) | collective-permute-done | bytes 65568 | tf_op jit(solution)/shard_map/while/body/eval_jaxpr/ppermute | solution.py:18
  290.1 6.2 %collective-permute-done.3 = f32[1,128,128]{2,1,0:T(8,128)S(1)} collective-permute-done((f32[1,128,128]{2,1,0:T(8,128)S(1)}, f32[1,128,128]{2,1,0:T(8,128)S(1)}, u32[]{:S(2)}, u32[]{:S(2)}) %collective-permute-start.3) | collective-permute-done | bytes 65568 | tf_op jit(solution)/shard_map/while/body/eval_jaxpr/ppermute | solution.py:18
  301.7 6.2 %collective-permute-done.3 = f32[1,128,128]{2,1,0:T(8,128)S(1)} collective-permute-done((f32[1,128,128]{2,1,0:T(8,128)S(1)}, f32[1,128,128]{2,1,0:T(8,128)S(1)}, u32[]{:S(2)}, u32[]{:S(2)}) %collective-permute-start.3) | collective-permute-done | bytes 65568 | tf_op jit(solution)/shard_map/while/body/eval_jaxpr/ppermute | solution.py:18
  336.5 6.4 %collective-permute-done.3 = f32[1,128,128]{2,1,0:T(8,128)S(1)} collective-permute-done((f32[1,128,128]{2,1,0:T(8,128)S(1)}, f32[1,128,128]{2,1,0:T(8,128)S(1)}, u32[]{:S(2)}, u32[]{:S(2)}) %collective-permute-start.3) | collective-permute-done | bytes 65568 | tf_op jit(solution)/shard_map/while/body/eval_jaxpr/ppermute | solution.py:18
  347.0 118.5 %while.62 = (s32[]{:T(128)}, f32[8,128,128]{2,1,0:T(8,128)S(1)}, f32[8,128,128]{2,1,0:T(8,128)S(1)}, f32[8,128,128]{2,1,0:T(8,128)S(1)}, s32[]{:T(128)}) while((s32[]{:T(128)}, f32[8,128,128]{2,1,0:T(8,128)S(1)}, f32[8,128,128]{2,1,0:T(8,128)S(1)}, f32[8,128,128]{2,1,0:T(8,128)S(1)}, s32[]{:T(128)}) %tuple.137), condition=%wide.region_8.9_spmd, body=%wide.region_7.8_spmd.sunk | while | flops 4238938 | bytes 8540461 | solution.py:75
  351.4 31.0 %collective-permute-done.5 = f32[1,128,128]{2,1,0:T(8,128)S(1)} collective-permute-done((f32[1,128,128]{2,1,0:T(8,128)S(1)}, f32[1,128,128]{2,1,0:T(8,128)S(1)}, u32[]{:S(2)}, u32[]{:S(2)}) %collective-permute-start.5) | collective-permute-done | bytes 65568 | tf_op jit(solution)/shard_map/while/body/eval_jaxpr/ppermute | solution.py:18
  434.3 6.2 %collective-permute-done.5 = f32[1,128,128]{2,1,0:T(8,128)S(1)} collective-permute-done((f32[1,128,128]{2,1,0:T(8,128)S(1)}, f32[1,128,128]{2,1,0:T(8,128)S(1)}, u32[]{:S(2)}, u32[]{:S(2)}) %collective-permute-start.5) | collective-permute-done | bytes 65568 | tf_op jit(solution)/shard_map/while/body/eval_jaxpr/ppermute | solution.py:18
  457.5 6.9 %collective-permute-done.5 = f32[1,128,128]{2,1,0:T(8,128)S(1)} collective-permute-done((f32[1,128,128]{2,1,0:T(8,128)S(1)}, f32[1,128,128]{2,1,0:T(8,128)S(1)}, u32[]{:S(2)}, u32[]{:S(2)}) %collective-permute-start.5) | collective-permute-done | bytes 65568 | tf_op jit(solution)/shard_map/while/body/eval_jaxpr/ppermute | solution.py:18
  467.5 63.4 %collective-permute-done.10 = f32[2,8,128,128]{3,2,1,0:T(8,128)S(1)} collective-permute-done((f32[2,8,128,128]{3,2,1,0:T(8,128)S(1)}, f32[2,8,128,128]{3,2,1,0:T(8,128)S(1)}, u32[]{:S(2)}, u32[]{:S(2)}) %collective-permute-start.10) | collective-permute-done | bytes 1048608 | tf_op jit(solution)/shard_map/ppermute | solution.py:30
  (311 shorter events, 310.5 us)
Async XLA Ops:
  8.2 14.7 %collective-permute-start.6 = (f32[1,128,128]{2,1,0:T(8,128)S(1)}, f32[1,128,128]{2,1,0:T(8,128)S(1)}, u32[]{:S(2)}, u32[]{:S(2)}) collective-permute-start(f32[1,128,128]{2,1,0:T(8,128)S(1)} %get-tuple-element.531), channel_id=1, source_target_pairs={{1,0},{2,1},{3,2},{4,3},{5,4},{6,5},{7,6},{8,7},{9,8},{10,9},{11,1... | collective-permute-start | bytes 196616 | tf_op jit(solution)/shard_map/while/body/eval_jaxpr/ppermute | solution.py:20
  14.0 8.8 %collective-permute-start.7 = (f32[1,128,128]{2,1,0:T(8,128)S(1)}, f32[1,128,128]{2,1,0:T(8,128)S(1)}, u32[]{:S(2)}, u32[]{:S(2)}) collective-permute-start(f32[1,128,128]{2,1,0:T(8,128)S(1)} %get-tuple-element.532), channel_id=1, source_target_pairs={{0,1},{1,2},{2,3},{3,4},{4,5},{5,6},{6,7},{7,8},{8,9},{9,10},{10,1... | collective-permute-start | bytes 196616 | tf_op jit(solution)/shard_map/while/body/eval_jaxpr/ppermute | solution.py:18
  24.0 15.4 %collective-permute-start.6 = (f32[1,128,128]{2,1,0:T(8,128)S(1)}, f32[1,128,128]{2,1,0:T(8,128)S(1)}, u32[]{:S(2)}, u32[]{:S(2)}) collective-permute-start(f32[1,128,128]{2,1,0:T(8,128)S(1)} %get-tuple-element.531), channel_id=1, source_target_pairs={{1,0},{2,1},{3,2},{4,3},{5,4},{6,5},{7,6},{8,7},{9,8},{10,9},{11,1... | collective-permute-start | bytes 196616 | tf_op jit(solution)/shard_map/while/body/eval_jaxpr/ppermute | solution.py:20
  30.6 8.8 %collective-permute-start.7 = (f32[1,128,128]{2,1,0:T(8,128)S(1)}, f32[1,128,128]{2,1,0:T(8,128)S(1)}, u32[]{:S(2)}, u32[]{:S(2)}) collective-permute-start(f32[1,128,128]{2,1,0:T(8,128)S(1)} %get-tuple-element.532), channel_id=1, source_target_pairs={{0,1},{1,2},{2,3},{3,4},{4,5},{5,6},{6,7},{7,8},{8,9},{9,10},{10,1... | collective-permute-start | bytes 196616 | tf_op jit(solution)/shard_map/while/body/eval_jaxpr/ppermute | solution.py:18
  40.6 15.4 %collective-permute-start.6 = (f32[1,128,128]{2,1,0:T(8,128)S(1)}, f32[1,128,128]{2,1,0:T(8,128)S(1)}, u32[]{:S(2)}, u32[]{:S(2)}) collective-permute-start(f32[1,128,128]{2,1,0:T(8,128)S(1)} %get-tuple-element.531), channel_id=1, source_target_pairs={{1,0},{2,1},{3,2},{4,3},{5,4},{6,5},{7,6},{8,7},{9,8},{10,9},{11,1... | collective-permute-start | bytes 196616 | tf_op jit(solution)/shard_map/while/body/eval_jaxpr/ppermute | solution.py:20
  47.2 8.8 %collective-permute-start.7 = (f32[1,128,128]{2,1,0:T(8,128)S(1)}, f32[1,128,128]{2,1,0:T(8,128)S(1)}, u32[]{:S(2)}, u32[]{:S(2)}) collective-permute-start(f32[1,128,128]{2,1,0:T(8,128)S(1)} %get-tuple-element.532), channel_id=1, source_target_pairs={{0,1},{1,2},{2,3},{3,4},{4,5},{5,6},{6,7},{7,8},{8,9},{9,10},{10,1... | collective-permute-start | bytes 196616 | tf_op jit(solution)/shard_map/while/body/eval_jaxpr/ppermute | solution.py:18
  57.2 15.4 %collective-permute-start.6 = (f32[1,128,128]{2,1,0:T(8,128)S(1)}, f32[1,128,128]{2,1,0:T(8,128)S(1)}, u32[]{:S(2)}, u32[]{:S(2)}) collective-permute-start(f32[1,128,128]{2,1,0:T(8,128)S(1)} %get-tuple-element.531), channel_id=1, source_target_pairs={{1,0},{2,1},{3,2},{4,3},{5,4},{6,5},{7,6},{8,7},{9,8},{10,9},{11,1... | collective-permute-start | bytes 196616 | tf_op jit(solution)/shard_map/while/body/eval_jaxpr/ppermute | solution.py:20
  63.8 8.8 %collective-permute-start.7 = (f32[1,128,128]{2,1,0:T(8,128)S(1)}, f32[1,128,128]{2,1,0:T(8,128)S(1)}, u32[]{:S(2)}, u32[]{:S(2)}) collective-permute-start(f32[1,128,128]{2,1,0:T(8,128)S(1)} %get-tuple-element.532), channel_id=1, source_target_pairs={{0,1},{1,2},{2,3},{3,4},{4,5},{5,6},{6,7},{7,8},{8,9},{9,10},{10,1... | collective-permute-start | bytes 196616 | tf_op jit(solution)/shard_map/while/body/eval_jaxpr/ppermute | solution.py:18
  73.8 15.4 %collective-permute-start.6 = (f32[1,128,128]{2,1,0:T(8,128)S(1)}, f32[1,128,128]{2,1,0:T(8,128)S(1)}, u32[]{:S(2)}, u32[]{:S(2)}) collective-permute-start(f32[1,128,128]{2,1,0:T(8,128)S(1)} %get-tuple-element.531), channel_id=1, source_target_pairs={{1,0},{2,1},{3,2},{4,3},{5,4},{6,5},{7,6},{8,7},{9,8},{10,9},{11,1... | collective-permute-start | bytes 196616 | tf_op jit(solution)/shard_map/while/body/eval_jaxpr/ppermute | solution.py:20
  80.4 8.8 %collective-permute-start.7 = (f32[1,128,128]{2,1,0:T(8,128)S(1)}, f32[1,128,128]{2,1,0:T(8,128)S(1)}, u32[]{:S(2)}, u32[]{:S(2)}) collective-permute-start(f32[1,128,128]{2,1,0:T(8,128)S(1)} %get-tuple-element.532), channel_id=1, source_target_pairs={{0,1},{1,2},{2,3},{3,4},{4,5},{5,6},{6,7},{7,8},{8,9},{9,10},{10,1... | collective-permute-start | bytes 196616 | tf_op jit(solution)/shard_map/while/body/eval_jaxpr/ppermute | solution.py:18
  90.4 15.4 %collective-permute-start.6 = (f32[1,128,128]{2,1,0:T(8,128)S(1)}, f32[1,128,128]{2,1,0:T(8,128)S(1)}, u32[]{:S(2)}, u32[]{:S(2)}) collective-permute-start(f32[1,128,128]{2,1,0:T(8,128)S(1)} %get-tuple-element.531), channel_id=1, source_target_pairs={{1,0},{2,1},{3,2},{4,3},{5,4},{6,5},{7,6},{8,7},{9,8},{10,9},{11,1... | collective-permute-start | bytes 196616 | tf_op jit(solution)/shard_map/while/body/eval_jaxpr/ppermute | solution.py:20
  97.0 8.8 %collective-permute-start.7 = (f32[1,128,128]{2,1,0:T(8,128)S(1)}, f32[1,128,128]{2,1,0:T(8,128)S(1)}, u32[]{:S(2)}, u32[]{:S(2)}) collective-permute-start(f32[1,128,128]{2,1,0:T(8,128)S(1)} %get-tuple-element.532), channel_id=1, source_target_pairs={{0,1},{1,2},{2,3},{3,4},{4,5},{5,6},{6,7},{7,8},{8,9},{9,10},{10,1... | collective-permute-start | bytes 196616 | tf_op jit(solution)/shard_map/while/body/eval_jaxpr/ppermute | solution.py:18
  107.0 15.4 %collective-permute-start.6 = (f32[1,128,128]{2,1,0:T(8,128)S(1)}, f32[1,128,128]{2,1,0:T(8,128)S(1)}, u32[]{:S(2)}, u32[]{:S(2)}) collective-permute-start(f32[1,128,128]{2,1,0:T(8,128)S(1)} %get-tuple-element.531), channel_id=1, source_target_pairs={{1,0},{2,1},{3,2},{4,3},{5,4},{6,5},{7,6},{8,7},{9,8},{10,9},{11,1... | collective-permute-start | bytes 196616 | tf_op jit(solution)/shard_map/while/body/eval_jaxpr/ppermute | solution.py:20
  113.6 8.8 %collective-permute-start.7 = (f32[1,128,128]{2,1,0:T(8,128)S(1)}, f32[1,128,128]{2,1,0:T(8,128)S(1)}, u32[]{:S(2)}, u32[]{:S(2)}) collective-permute-start(f32[1,128,128]{2,1,0:T(8,128)S(1)} %get-tuple-element.532), channel_id=1, source_target_pairs={{0,1},{1,2},{2,3},{3,4},{4,5},{5,6},{6,7},{7,8},{8,9},{9,10},{10,1... | collective-permute-start | bytes 196616 | tf_op jit(solution)/shard_map/while/body/eval_jaxpr/ppermute | solution.py:18
  123.6 15.4 %collective-permute-start.6 = (f32[1,128,128]{2,1,0:T(8,128)S(1)}, f32[1,128,128]{2,1,0:T(8,128)S(1)}, u32[]{:S(2)}, u32[]{:S(2)}) collective-permute-start(f32[1,128,128]{2,1,0:T(8,128)S(1)} %get-tuple-element.531), channel_id=1, source_target_pairs={{1,0},{2,1},{3,2},{4,3},{5,4},{6,5},{7,6},{8,7},{9,8},{10,9},{11,1... | collective-permute-start | bytes 196616 | tf_op jit(solution)/shard_map/while/body/eval_jaxpr/ppermute | solution.py:20
  140.2 9.2 %collective-permute-start = (f32[1,128,128]{2,1,0:T(8,128)S(1)}, f32[1,128,128]{2,1,0:T(8,128)S(1)}, u32[]{:S(2)}, u32[]{:S(2)}) collective-permute-start(f32[1,128,128]{2,1,0:T(8,128)S(1)} %get-tuple-element.511), channel_id=1, source_target_pairs={{1,0},{2,1},{3,2},{4,3},{5,4},{6,5},{7,6},{8,7},{9,8},{10,9},{11,1... | collective-permute-start | bytes 196616 | tf_op jit(solution)/shard_map/while/body/eval_jaxpr/ppermute | solution.py:20
  228.2 8.8 %collective-permute-start.1 = (f32[1,128,128]{2,1,0:T(8,128)S(1)}, f32[1,128,128]{2,1,0:T(8,128)S(1)}, u32[]{:S(2)}, u32[]{:S(2)}) collective-permute-start(f32[1,128,128]{2,1,0:T(8,128)S(1)} %get-tuple-element.512), channel_id=1, source_target_pairs={{0,1},{1,2},{2,3},{3,4},{4,5},{5,6},{6,7},{7,8},{8,9},{9,10},{10,1... | collective-permute-start | bytes 196616 | tf_op jit(solution)/shard_map/while/body/eval_jaxpr/ppermute | solution.py:18
  239.1 228.4 %collective-permute-start.8 = (f32[2,8,128,128]{3,2,1,0:T(8,128)}, f32[2,8,128,128]{3,2,1,0:T(8,128)}, u32[]{:S(2)}, u32[]{:S(2)}) collective-permute-start(f32[2,8,128,128]{3,2,1,0:T(8,128)} %pad_maximum_fusion.8), channel_id=1, source_target_pairs={{0,32},{32,64},{64,96},{96,128},{128,160},{160,192},{192,224},{224... | collective-permute-start | bytes 3145736 | tf_op jit(solution)/shard_map/ppermute | solution.py:30
  243.0 18.4 %collective-permute-start.3 = (f32[1,128,128]{2,1,0:T(8,128)S(1)}, f32[1,128,128]{2,1,0:T(8,128)S(1)}, u32[]{:S(2)}, u32[]{:S(2)}) collective-permute-start(f32[1,128,128]{2,1,0:T(8,128)S(1)} %get-tuple-element.518), channel_id=1, source_target_pairs={{0,1},{1,2},{2,3},{3,4},{4,5},{5,6},{6,7},{7,8},{8,9},{9,10},{10,1... | collective-permute-start | bytes 196616 | tf_op jit(solution)/shard_map/while/body/eval_jaxpr/ppermute | solution.py:18
  334.1 8.9 %collective-permute-start.3 = (f32[1,128,128]{2,1,0:T(8,128)S(1)}, f32[1,128,128]{2,1,0:T(8,128)S(1)}, u32[]{:S(2)}, u32[]{:S(2)}) collective-permute-start(f32[1,128,128]{2,1,0:T(8,128)S(1)} %get-tuple-element.518), channel_id=1, source_target_pairs={{0,1},{1,2},{2,3},{3,4},{4,5},{5,6},{6,7},{7,8},{8,9},{9,10},{10,1... | collective-permute-start | bytes 196616 | tf_op jit(solution)/shard_map/while/body/eval_jaxpr/ppermute | solution.py:18
  345.1 122.5 %collective-permute-start.9 = (f32[2,8,128,128]{3,2,1,0:T(8,128)}, f32[2,8,128,128]{3,2,1,0:T(8,128)}, u32[]{:S(2)}, u32[]{:S(2)}) collective-permute-start(f32[2,8,128,128]{3,2,1,0:T(8,128)} %pad_maximum_fusion.9), channel_id=1, source_target_pairs={{0,64},{32,96},{64,128},{96,160},{128,192},{160,224},{192,256},{22... | collective-permute-start | bytes 3145736 | tf_op jit(solution)/shard_map/ppermute | solution.py:30
  348.9 33.5 %collective-permute-start.5 = (f32[1,128,128]{2,1,0:T(8,128)S(1)}, f32[1,128,128]{2,1,0:T(8,128)S(1)}, u32[]{:S(2)}, u32[]{:S(2)}) collective-permute-start(f32[1,128,128]{2,1,0:T(8,128)S(1)} %get-tuple-element.524), channel_id=1, source_target_pairs={{0,1},{1,2},{2,3},{3,4},{4,5},{5,6},{6,7},{7,8},{8,9},{9,10},{10,1... | collective-permute-start | bytes 196616 | tf_op jit(solution)/shard_map/while/body/eval_jaxpr/ppermute | solution.py:18
  455.1 9.3 %collective-permute-start.5 = (f32[1,128,128]{2,1,0:T(8,128)S(1)}, f32[1,128,128]{2,1,0:T(8,128)S(1)}, u32[]{:S(2)}, u32[]{:S(2)}) collective-permute-start(f32[1,128,128]{2,1,0:T(8,128)S(1)} %get-tuple-element.524), channel_id=1, source_target_pairs={{0,1},{1,2},{2,3},{3,4},{4,5},{5,6},{6,7},{7,8},{8,9},{9,10},{10,1... | collective-permute-start | bytes 196616 | tf_op jit(solution)/shard_map/while/body/eval_jaxpr/ppermute | solution.py:18
  465.6 65.3 %collective-permute-start.10 = (f32[2,8,128,128]{3,2,1,0:T(8,128)S(1)}, f32[2,8,128,128]{3,2,1,0:T(8,128)S(1)}, u32[]{:S(2)}, u32[]{:S(2)}) collective-permute-start(f32[2,8,128,128]{3,2,1,0:T(8,128)S(1)} %pad_maximum_fusion.10), channel_id=1, source_target_pairs={{0,96},{32,128},{64,160},{96,192},{128,224},{160,256},{192,288},{2... | collective-permute-start | bytes 3145736 | tf_op jit(solution)/shard_map/ppermute | solution.py:30
  (44 other events, 280.6 us)
where the time goes:
time: 536 us; the launch traced here: 534 us
  waiting for transfers between devices  248 us (46%)
  starting transfers between devices  182 us (34%)
  other arithmetic  91.2 us (17%)
  local copies, waits for them, and re-layouts  10.3 us (2%)
    ppermute x32, waiting for transfers between devices, extended(): lax.ppermute(tail, axis, [(i, (i + 1) % count) for i in range(ends)])  183 us
    ppermute x32, starting transfers between devices, extended(): lax.ppermute(head, axis, [((i + 1) % count, i) for i in range(ends)])  103 us
    ppermute x32, starting transfers between devices, extended(): lax.ppermute(tail, axis, [(i, (i + 1) % count) for i in range(ends)])  72.6 us
    ppermute x3, waiting for transfers between devices, passed_along(): return lax.ppermute(block, axis, route)  63.4 us
    scatter-add x8, other arithmetic, make_forcing(): return jnp.zeros((slab_cells,), jnp.float32).at[source_cell].add(wavelet_...  48.4 us
    add x32, other arithmetic, leap_step(): newest = 2.0 * current - earlier + courant * laplace(current) + forcing  17.3 us
    concatenate x32, other arithmetic, extended(): jnp.concatenate([lax.ppermute(tail, axis, [(i, (i + 1) % count) for i in...  13.6 us
  transfers between devices with their start and end apart: 67, of which 33 were waited for; matrix products, arithmetic and copies ran while one was open for 14% of the time, Pallas kernels for 0%

commit v1 on v0

v1 whole, which is shorter than its diff:
```python
import functools

import jax
import jax.numpy as jnp
from jax import lax
from jax.experimental import pallas as pl
from jax.experimental.pallas import tpu as pltpu
from jax.sharding import PartitionSpec as P

MESH = pl.DeviceIdType.MESH
STEPS = 8
SPAN = 3
ROUNDS = SPAN + 1
GHOST = 4
PIECES = 3
ROW0 = 8


def kernel(
    tms, spaces,
    region_ref, coef_ref, cell_ref, amp_ref, out_ref,
    u, v, co, hist, send, force, rows_hot, cols_hot, amps, pieces,
    amp_send, amp_recv, co_send, co_recv, plane_send, plane_recv,
):
    t, s = lax.axis_index("tm"), lax.axis_index("space")
    cz, nx, ny = region_ref.shape
    own = GHOST + 1
    has = (s > 0, s < spaces - 1)
    beside = ({"space": s - 1}, {"space": s + 1})

    barrier = pltpu.get_barrier_semaphore()
    expected = 0
    partners = [(has[0], beside[0]), (has[1], beside[1])]
    for m in range(1, SPAN + 1):
        partners.append((t - m >= 0, {"tm": t - m}))
        partners.append((t + m < tms, {"tm": t + m}))
    for there, device in partners:
        @pl.when(there)
        def _(device=device):
            pl.semaphore_signal(barrier, inc=1, device_id=device, device_id_type=MESH)
        expected = expected + jnp.where(there, 1, 0)

    def courant_plane(z, _):
        region = region_ref[z]
        value = jnp.zeros((nx, ny), jnp.float32)
        for i in range(coef_ref.shape[0]):
            value = jnp.where(region == i, coef_ref[i], value)
        co[own + z] = value
        return 0

    lax.fori_loop(0, cz, courant_plane, 0)
    zero_plane = jnp.zeros((nx, ny), jnp.float32)

    def clear_u(p, _):
        for i in range(2):
            u[i, p] = jnp.zeros(u.shape[2:], jnp.float32)
        return 0

    def clear_v(z, _):
        for i in range(2):
            v[i, z] = jnp.zeros(v.shape[2:], jnp.float32)
        return 0

    lax.fori_loop(0, u.shape[1], clear_u, 0)
    lax.fori_loop(0, cz, clear_v, 0)
    for m in range(1, SPAN + 1):
        @pl.when(t - m < 0)
        def _(m=m):
            amps[m - 1] = jnp.zeros(amps.shape[1:], jnp.float32)
    for side in range(2):
        @pl.when(jnp.logical_not(has[side]))
        def _(side=side):
            for d in range(GHOST):
                co[own - 1 - d if side == 0 else own + cz + d] = zero_plane

            def clear_hist(i, _):
                hist[i // STEPS, lax.rem(i, STEPS), side] = zero_plane
                return 0

            lax.fori_loop(0, ROUNDS * STEPS, clear_hist, 0)

    pl.semaphore_wait(barrier, expected)

    def amp_copy(m):
        return pltpu.make_async_remote_copy(
            amp_ref.at[0], amps.at[m - 1], amp_send.at[m - 1], amp_recv.at[m - 1],
            device_id={"tm": t + m}, device_id_type=MESH)

    for m in range(SPAN, 0, -1):
        @pl.when(t + m < tms)
        def _(m=m):
            amp_copy(m).start()

    def co_copy(side, d):
        source = own + d if side == 0 else own + cz - 1 - d
        target = own + cz + d if side == 0 else own - 1 - d
        return pltpu.make_async_remote_copy(
            co.at[source], co.at[target], co_send.at[side, d], co_recv.at[1 - side, d],
            device_id=beside[side], device_id_type=MESH)

    def co_wait(side, d):
        target = own - 1 - d if side == 0 else own + cz + d
        return pltpu.make_async_remote_copy(
            co.at[target], co.at[target], co_send.at[side, d], co_recv.at[side, d],
            device_id=beside[side], device_id_type=MESH)

    for d in range(GHOST):
        for side in range(2):
            @pl.when(has[side])
            def _(side=side, d=d):
                co_copy(side, d).start()

    def plane_copy(r, k, side):
        return pltpu.make_async_remote_copy(
            send.at[r, k, side], hist.at[r, k, 1 - side], plane_send.at[r, k, side], plane_recv.at[r, k, 1 - side],
            device_id=beside[side], device_id_type=MESH)

    def plane_wait(r, k, side):
        return pltpu.make_async_remote_copy(
            send.at[r, k, side], hist.at[r, k, side], plane_send.at[r, k, side], plane_recv.at[r, k, side],
            device_id=beside[side], device_id_type=MESH)

    def send_planes(r, k):
        for side in range(2):
            @pl.when(has[side])
            def _(side=side):
                plane_copy(r, k, side).start()

    def await_planes(r, k):
        for side in range(2):
            @pl.when(has[side])
            def _(side=side):
                plane_wait(r, k, side).wait_recv()

    def rows_block(i, _):
        cell = cell_ref[...]
        row = cell // ny
        rows = 64
        index = lax.broadcasted_iota(jnp.int32, (rows, cell.shape[1]), 0) + i * rows
        rows_hot[pl.ds(pl.multiple_of(i * rows, rows), rows), :] = jnp.where(row == index, 1.0, 0.0).astype(jnp.bfloat16)
        return 0

    lax.fori_loop(0, cz * nx // 64, rows_block, 0)

    def cols_block(i, _):
        col = lax.rem(cell_ref[...], ny)
        rows = 64
        index = lax.broadcasted_iota(jnp.int32, (rows, col.shape[1]), 0) + i * rows
        cols_hot[pl.ds(pl.multiple_of(i * rows, rows), rows), :] = jnp.where(col == index, 1.0, 0.0).astype(jnp.bfloat16)
        return 0

    lax.fori_loop(0, ny // 64, cols_block, 0)

    def split_amplitude(slot, value):
        for piece in range(PIECES):
            part = value.astype(jnp.bfloat16)
            pieces[slot, piece] = part.astype(jnp.float32)
            value = value - part.astype(jnp.float32)

    def make_force(slot, n):
        weights = []
        for piece in range(PIECES):
            a = pieces[slot, piece, pl.ds(n, 1), :].astype(jnp.bfloat16)
            weights.append(cols_hot[...] * a)

        rows = 256

        def block(i, _):
            at = pl.ds(pl.multiple_of(i * rows, rows), rows)
            hot = rows_hot[at, :]
            total = None
            for w in weights:
                part = lax.dot_general(hot, w, (((1,), (1,)), ((), ())), preferred_element_type=jnp.float32)
                total = part if total is None else total + part
            force[n, at, :] = total
            return 0

        lax.fori_loop(0, cz * nx // rows, block, 0)

    lane = lax.broadcasted_iota(jnp.int32, (8, ny), 1)
    first_lane, last_lane = lane == 0, lane == ny - 1

    def stencil(c, above, below, up, down, earlier, speed):
        left = jnp.where(first_lane, 0.0, pltpu.roll(c, 1, axis=1))
        right = jnp.where(last_lane, 0.0, pltpu.roll(c, ny - 1, axis=1))
        around = (above + below) + (up + down) + (left + right)
        return (c + c) - earlier + speed * (around - 6.0 * c)

    def run_alone(r, k):
        now, later = (k - 1) % 2, k % 2
        depth = min(k, STEPS - k)

        def block(i, _):
            x = pl.multiple_of(i * 8, 8)
            rows = pl.ds(x + ROW0, 8)
            before = u[now, own - depth - 1, rows, :]
            c = u[now, own - depth, rows, :]
            for z in range(-depth, cz + depth):
                p = own + z
                after = u[now, p + 1, rows, :]
                new = stencil(
                    c, before, after,
                    u[now, p, pl.ds(x + ROW0 - 1, 8), :], u[now, p, pl.ds(x + ROW0 + 1, 8), :],
                    u[later, p, rows, :], co[p, pl.ds(x, 8), :])
                if 0 <= z < cz:
                    new = new + force[k - 1, pl.ds(z * nx + x, 8), :]
                u[later, p, rows, :] = new
                if k < STEPS and z == 0:
                    send[r, k, 0, pl.ds(x, 8), :] = new
                if k < STEPS and z == cz - 1:
                    send[r, k, 1, pl.ds(x, 8), :] = new
                before, c = c, after
            return 0

        lax.fori_loop(0, nx // 8, block, 0)

    def run_caused(r, k):
        now, later = (k - 1) % 2, k % 2
        if k < cz // 2:
            groups = [range(0, k), range(cz - k, cz)]
        else:
            groups = [range(0, cz)]

        def block(i, _):
            x = pl.multiple_of(i * 8, 8)
            rows = pl.ds(x + ROW0, 8)
            at = pl.ds(x, 8)

            def plane(z):
                if z < 0:
                    return hist[r, k - 1, 0, at, :]
                if z >= cz:
                    return hist[r, k - 1, 1, at, :]
                return v[now, z, rows, :]

            for group in groups:
                before, c = plane(group[0] - 1), plane(group[0])
                for z in group:
                    after = plane(z + 1)
                    new = stencil(
                        c, before, after,
                        v[now, z, pl.ds(x + ROW0 - 1, 8), :], v[now, z, pl.ds(x + ROW0 + 1, 8), :],
                        v[later, z, rows, :], co[own + z, at, :])
                    if k < STEPS:
                        v[later, z, rows, :] = new
                    if k >= STEPS - 1:
                        whole = u[later, own + z, rows, :] + new
                        u[later, own + z, rows, :] = whole
                        if k == STEPS and z in (0, cz - 1):
                            side = 0 if z == 0 else 1
                            send[lax.rem(r + 1, ROUNDS), 0, side, at, :] = whole
                    before, c = c, after
            return 0

        lax.fori_loop(0, nx // 8, block, 0)

    for m in range(SPAN, 0, -1):
        @pl.when(t - m >= 0)
        def _(m=m):
            amp_copy(m).wait_recv()
        split_amplitude(SPAN - m, amps[m - 1])
    split_amplitude(SPAN, amp_ref[0])

    def one_round(r, _):
        @pl.when(r > 0)
        def _():
            send_planes(r, 0)

            def clear(d, _):
                for i in range(2):
                    u[i, own - 1 - d] = jnp.zeros(u.shape[2:], jnp.float32)
                    u[i, own + cz + d] = jnp.zeros(u.shape[2:], jnp.float32)
                return 0

            lax.fori_loop(0, GHOST, clear, 0)
            lax.fori_loop(0, cz, clear_v, 0)

        for k in range(1, STEPS + 1):
            @pl.when(r == 0)
            def _(k=k):
                make_force(0, k - 1)
                if k <= GHOST:
                    for side in range(2):
                        @pl.when(has[side])
                        def _(side=side):
                            co_wait(side, k - 1).wait_recv()

            run_alone(r, k)
            if k < STEPS:
                send_planes(r, k)
        for k in range(1, STEPS + 1):
            if k == 1:
                @pl.when(r > 0)
                def _():
                    await_planes(r, 0)
                    run_caused(r, 1)
            else:
                await_planes(r, k - 1)
                run_caused(r, k)

            @pl.when(r < SPAN)
            def _(k=k):
                make_force(r + 1, k - 1)
        return 0

    lax.fori_loop(0, ROUNDS, one_round, 0)

    for i in range(2):
        def copy_out(z, _):
            out_ref[0, i, z] = u[1 - i, own + z, ROW0:ROW0 + nx, :]
            return 0
        lax.fori_loop(0, cz, copy_out, 0)

    for m in range(1, SPAN + 1):
        @pl.when(t + m < tms)
        def _(m=m):
            amp_copy(m).wait_send()
    for side in range(2):
        @pl.when(has[side])
        def _(side=side):
            for d in range(GHOST):
                co_copy(side, d).wait_send()

            def drain(i, _):
                plane_copy(i // STEPS, lax.rem(i, STEPS), side).wait_send()
                return 0

            lax.fori_loop(1, ROUNDS * STEPS, drain, 0)


def solution(mesh):
    tms, spaces = mesh.shape["tm"], mesh.shape["space"]

    def shards(region_map, region_coef, source_cell, amplitude):
        cz, nx, ny = region_map.shape
        sources = source_cell.shape[0]
        planes = cz + 2 * GHOST + 2
        return pl.pallas_call(
            functools.partial(kernel, tms, spaces),
            out_shape=jax.ShapeDtypeStruct((1, 2, cz, nx, ny), jnp.float32),
            in_specs=[
                pl.BlockSpec(memory_space=pltpu.VMEM),
                pl.BlockSpec(memory_space=pltpu.SMEM),
                pl.BlockSpec(memory_space=pltpu.VMEM),
                pl.BlockSpec(memory_space=pltpu.VMEM),
            ],
            out_specs=pl.BlockSpec(memory_space=pltpu.VMEM),
            scratch_shapes=[
                pltpu.VMEM((2, planes, nx + 2 * ROW0, ny), jnp.float32),
                pltpu.VMEM((2, cz, nx + 2 * ROW0, ny), jnp.float32),
                pltpu.VMEM((planes, nx, ny), jnp.float32),
                pltpu.VMEM((ROUNDS, STEPS, 2, nx, ny), jnp.float32),
                pltpu.VMEM((ROUNDS, STEPS, 2, nx, ny), jnp.float32),
                pltpu.VMEM((STEPS, cz * nx, ny), jnp.float32),
                pltpu.VMEM((cz * nx, sources), jnp.bfloat16),
                pltpu.VMEM((ny, sources), jnp.bfloat16),
                pltpu.VMEM((SPAN, STEPS, sources), jnp.float32),
                pltpu.VMEM((ROUNDS, PIECES, STEPS, sources), jnp.float32),
                pltpu.SemaphoreType.DMA((SPAN,)),
                pltpu.SemaphoreType.DMA((SPAN,)),
                pltpu.SemaphoreType.DMA((2, GHOST)),
                pltpu.SemaphoreType.DMA((2, GHOST)),
                pltpu.SemaphoreType.DMA((ROUNDS, STEPS, 2)),
                pltpu.SemaphoreType.DMA((ROUNDS, STEPS, 2)),
            ],
            compiler_params=pltpu.CompilerParams(
                collective_id=0, has_side_effects=True, vmem_limit_bytes=60 << 20
            ),
        )(region_map, region_coef, source_cell.reshape(1, sources), amplitude)

    placed = (P("space", None, None), P(), P("space"), P("tm", None, "space"))
    return jax.shard_map(
        shards, mesh=mesh, in_specs=placed, out_specs=P("tm", None, "space", None, None), check_vma=False
    )
```

time: 536 us -> 198 us (0.37)
  the two profiles are of different devices: /device:TPU:454 before, /device:TPU:12 now
where the time goes in v1:
time: 198 us
  Pallas kernels  195 us (98%)
  local copies, waits for them, and re-layouts  2.3 us (1%)
    pallas_call x1, Pallas kernels, shards(): pl.pallas_call(functools.partial(kernel, tms, spaces), out_shape=jax.Shap...  195 us

profile of v1, /device:TPU:12, one launch (start us, length us, event | category | flops | bytes accessed | tf_op | source)
XLA Modules:
  0.0 197.6 jit_solution(15225342578856153410)
XLA Ops:
  0.0 195.3 %shard_map.46 = f32[1,2,8,128,128]{4,3,2,1,0:T(8,128)} custom-call(s32[8,128,128]{2,1,0:T(8,128)} %region_ref.1, f32[8]{0:T(128)} %coef_ref.1, s32[1,1024]{1,0:T(1,128)} %bitcast.1, f32[1,8,1024]{2,1,0:T(8,128)} %amp_ref.1), custom_call_target="tpu_custom_call" | custom-call | tf_op jit(solution)/shard_map/pallas_call | solution.py:338
  195.3 2.3 %copy.6 = f32[1,2,8,128,128]{4,3,2,1,0:T(8,128)} copy(f32[1,2,8,128,128]{4,3,2,1,0:T(8,128)} %shard_map.46) | data formatting | bytes 2097152

commit v2 on v1

v2 whole, which is shorter than its diff:
```python
import functools

import jax
import jax.numpy as jnp
from jax import lax
from jax.experimental import pallas as pl
from jax.experimental.pallas import tpu as pltpu
from jax.sharding import PartitionSpec as P

MESH = pl.DeviceIdType.MESH
STEPS = 8
SPAN = 3
ROUNDS = SPAN + 1
GHOST = 4
FIRST = 2
PIECES = 2
ROW0 = 8


def kernel(
    tms, spaces,
    region_in, coef_in, cell_in, amp_in, out_ref,
    region_ref, coef_ref, cell_ref, amp_ref,
    u, v, co, hist, send, force, rows_hot, cols_hot, amps, pieces,
    local_sem, out_sem, amp_send, amp_recv, co_send, co_recv, plane_send, plane_recv,
):
    t, s = lax.axis_index("tm"), lax.axis_index("space")
    cz, nx, ny = region_in.shape
    own = GHOST + 1
    has = (s > 0, s < spaces - 1)
    beside = ({"space": s - 1}, {"space": s + 1})

    barrier = pltpu.get_barrier_semaphore()
    expected = 0
    partners = [(has[0], beside[0]), (has[1], beside[1])]
    for m in range(1, SPAN + 1):
        partners.append((t - m >= 0, {"tm": t - m}))
        partners.append((t + m < tms, {"tm": t + m}))
    for there, device in partners:
        @pl.when(there)
        def _(device=device):
            pl.semaphore_signal(barrier, inc=1, device_id=device, device_id_type=MESH)
        expected = expected + jnp.where(there, 1, 0)

    loads = [
        pltpu.make_async_copy(region_in, region_ref, local_sem.at[0]),
        pltpu.make_async_copy(coef_in, coef_ref, local_sem.at[1]),
        pltpu.make_async_copy(amp_in.at[0], amp_ref, local_sem.at[2]),
        pltpu.make_async_copy(cell_in, cell_ref, local_sem.at[3]),
    ]
    for load in loads:
        load.start()

    loads[0].wait()
    loads[1].wait()
    for z in range(cz):
        region = region_ref[z]
        value = jnp.zeros((nx, ny), jnp.float32)
        for i in range(coef_ref.shape[0]):
            value = jnp.where(region == i, coef_ref[i], value)
        co[own + z] = value
    zero_plane = jnp.zeros((nx, ny), jnp.float32)
    loads[2].wait()
    pl.semaphore_wait(barrier, expected)

    halves = (pl.ds(0, FIRST), pl.ds(FIRST, STEPS - FIRST))

    def amp_copy(m, part):
        return pltpu.make_async_remote_copy(
            amp_ref.at[halves[part]], amps.at[m - 1, halves[part]], amp_send.at[m - 1, part], amp_recv.at[m - 1, part],
            device_id={"tm": t + m}, device_id_type=MESH)

    @pl.when(t + SPAN < tms)
    def _():
        for part in range(2):
            amp_copy(SPAN, part).start()

    def co_copy(side, d):
        source = own + d if side == 0 else own + cz - 1 - d
        target = own + cz + d if side == 0 else own - 1 - d
        return pltpu.make_async_remote_copy(
            co.at[source], co.at[target], co_send.at[side, d], co_recv.at[1 - side, d],
            device_id=beside[side], device_id_type=MESH)

    def co_wait(side, d):
        target = own - 1 - d if side == 0 else own + cz + d
        return pltpu.make_async_remote_copy(
            co.at[target], co.at[target], co_send.at[side, d], co_recv.at[side, d],
            device_id=beside[side], device_id_type=MESH)

    for d in range(GHOST):
        for side in range(2):
            @pl.when(has[side])
            def _(side=side, d=d):
                co_copy(side, d).start()

    def plane_copy(r, k, side):
        return pltpu.make_async_remote_copy(
            send.at[r, k, side], hist.at[r, k, 1 - side], plane_send.at[r, k, side], plane_recv.at[r, k, 1 - side],
            device_id=beside[side], device_id_type=MESH)

    def plane_wait(r, k, side):
        return pltpu.make_async_remote_copy(
            send.at[r, k, side], hist.at[r, k, side], plane_send.at[r, k, side], plane_recv.at[r, k, side],
            device_id=beside[side], device_id_type=MESH)

    def send_planes(r, k):
        for side in range(2):
            @pl.when(has[side])
            def _(side=side):
                plane_copy(r, k, side).start()

    def await_planes(r, k):
        for side in range(2):
            @pl.when(has[side])
            def _(side=side):
                plane_wait(r, k, side).wait_recv()

    def clear_u(p, _):
        for i in range(2):
            u[i, p] = jnp.zeros(u.shape[2:], jnp.float32)
        return 0

    def clear_v(z, _):
        for i in range(2):
            v[i, z] = jnp.zeros(v.shape[2:], jnp.float32)
        return 0

    lax.fori_loop(0, u.shape[1], clear_u, 0)
    lax.fori_loop(0, cz, clear_v, 0)
    for m in range(1, SPAN + 1):
        @pl.when(t - m < 0)
        def _(m=m):
            amps[m - 1] = jnp.zeros(amps.shape[1:], jnp.float32)
    for side in range(2):
        @pl.when(jnp.logical_not(has[side]))
        def _(side=side):
            for d in range(GHOST):
                co[own - 1 - d if side == 0 else own + cz + d] = zero_plane

            def clear_hist(i, _):
                hist[i // STEPS, lax.rem(i, STEPS), side] = zero_plane
                return 0

            lax.fori_loop(0, ROUNDS * STEPS, clear_hist, 0)

    half = cz // 2 * nx
    loads[3].wait()

    def rows_block(i, _):
        row = lax.rem(cell_ref[...] // ny, half)
        rows = 64
        index = lax.broadcasted_iota(jnp.int32, (rows, row.shape[1]), 0) + i * rows
        rows_hot[pl.ds(pl.multiple_of(i * rows, rows), rows), :] = jnp.where(row == index, 1.0, 0.0).astype(jnp.bfloat16)
        return 0

    lax.fori_loop(0, half // 64, rows_block, 0)
    sources = cell_ref.shape[1]
    for i in range(sources // 128):
        cell = jnp.broadcast_to(cell_ref[:, i * 128:(i + 1) * 128], (128, 128)).T
        col = cell // (half * ny) * ny + lax.rem(cell, ny)
        col = jnp.concatenate([col] * (2 * ny // 128), axis=1)
        index = lax.broadcasted_iota(jnp.int32, col.shape, 1)
        cols_hot[i * 128:(i + 1) * 128, :] = jnp.where(col == index, 1.0, 0.0).astype(jnp.bfloat16)

    def split_amplitude(slot, value, part):
        for piece in range(PIECES):
            rounded = value.astype(jnp.bfloat16).astype(jnp.float32)
            pieces[slot, piece, halves[part], :] = rounded
            value = value - rounded

    def take_amplitude(m, part):
        @pl.when(t - m >= 0)
        def _():
            amp_copy(m, part).wait_recv()

        split_amplitude(SPAN - m, amps[m - 1, halves[part], :], part)

    def make_force(slot, n):
        total = None
        for piece in range(PIECES):
            a = pieces[slot, piece, pl.ds(n, 1), :].astype(jnp.bfloat16)
            part = jnp.dot(rows_hot[...] * a, cols_hot[...], preferred_element_type=jnp.float32)
            total = part if total is None else total + part
        for z in range(cz):
            at, side = z % (cz // 2) * nx, z // (cz // 2) * ny
            force[n % 2, z] = total[at:at + nx, side:side + ny]

    lane = lax.broadcasted_iota(jnp.int32, (nx, ny), 1)
    first_lane, last_lane = lane == 0, lane == ny - 1
    inner = pl.ds(ROW0, nx)

    def advance(field, now, later, p, speed, above, below, live, old):
        around = [x for x in (above, below) if x is not None]
        around = functools.reduce(jnp.add, around) if around else None
        if not live:
            return speed * around
        c = field[now, p, inner, :]
        beside_x = field[now, p, pl.ds(ROW0 - 1, nx), :] + field[now, p, pl.ds(ROW0 + 1, nx), :]
        left = jnp.where(first_lane, 0.0, pltpu.roll(c, 1, axis=1))
        right = jnp.where(last_lane, 0.0, pltpu.roll(c, ny - 1, axis=1))
        near = beside_x + (left + right)
        around = near if around is None else around + near
        base = c + c
        if old:
            base = base - field[later, p, inner, :]
        return base + speed * (around - 6.0 * c)

    def run_alone(r, k):
        now, later = (k - 1) % 2, k % 2
        depth = min(k, STEPS - k)

        def outside(z):
            return max(-z, z - cz + 1)

        def at(z):
            return u[now, own + z, inner, :] if outside(z) <= k - 1 else None

        for z in range(-depth, cz + depth):
            new = advance(u, now, later, own + z, co[own + z], at(z - 1), at(z + 1), outside(z) <= k - 1, outside(z) <= max(k - 2, 0))
            if 0 <= z < cz:
                new = new + force[(k - 1) % 2, z]
            u[later, own + z, inner, :] = new
            if k < STEPS and z == 0:
                send[r, k, 0] = new
            if k < STEPS and z == cz - 1:
                send[r, k, 1] = new

    def run_caused(r, k, planes):
        now, later = (k - 1) % 2, k % 2

        def inside(z):
            return min(z + 1, cz - z)

        def at(z):
            if z < 0:
                return hist[r, k - 1, 0]
            if z >= cz:
                return hist[r, k - 1, 1]
            return v[now, z, inner, :] if inside(z) <= k - 1 else None

        for z in planes:
            if inside(z) > k:
                continue
            new = advance(v, now, later, z, co[own + z], at(z - 1), at(z + 1), inside(z) <= k - 1, inside(z) <= k - 2)
            if k < STEPS:
                v[later, z, inner, :] = new
            if k >= STEPS - 1:
                whole = u[later, own + z, inner, :] + new
                u[later, own + z, inner, :] = whole
                if k == STEPS and z in (0, cz - 1):
                    send[lax.rem(r + 1, ROUNDS), 0, 0 if z == 0 else 1] = whole

    for part in range(2):
        split_amplitude(SPAN, amp_ref[halves[part], :], part)

    out_copies = [
        pltpu.make_async_copy(u.at[1 - i, pl.ds(own, cz), inner, :], out_ref.at[0, i], out_sem.at[i]) for i in range(2)
    ]

    def one_round(r, _):
        for m in range(1, SPAN):
            @pl.when(r == SPAN - m)
            def _(m=m):
                for part in range(2):
                    take_amplitude(m, part)

        for k in range(1, STEPS + 1):
            @pl.when(r == 0)
            def _(k=k):
                if k == 1:
                    take_amplitude(SPAN, 0)
                if k == FIRST + 1:
                    take_amplitude(SPAN, 1)
                if k == STEPS // 2:
                    for m in range(SPAN - 1, 0, -1):
                        @pl.when(t + m < tms)
                        def _(m=m):
                            for part in range(2):
                                amp_copy(m, part).start()
                if k <= GHOST:
                    for side in range(2):
                        @pl.when(has[side])
                        def _(side=side):
                            co_wait(side, k - 1).wait_recv()

            make_force(r, k - 1)
            run_alone(r, k)
            if k < STEPS:
                send_planes(r, k)
        for k in range(1, STEPS + 1):
            if k == 1:
                @pl.when(r > 0)
                def _():
                    await_planes(r, 0)
                    run_caused(r, 1, range(cz))

                @pl.when(r == 0)
                def _():
                    for z in (0, cz - 1):
                        v[1, z, inner, :] = zero_plane
            elif k < STEPS:
                await_planes(r, k - 1)
                run_caused(r, k, range(cz))
                if k == STEPS - 1:
                    @pl.when(r == SPAN)
                    def _():
                        out_copies[0].start()
            else:
                await_planes(r, k - 1)
                run_caused(r, k, (0, cz - 1))

                @pl.when(r < SPAN)
                def _():
                    send_planes(r + 1, 0)

                run_caused(r, k, range(1, cz - 1))
        return 0

    lax.fori_loop(0, ROUNDS, one_round, 0)

    out_copies[1].start()
    for m in range(1, SPAN + 1):
        @pl.when(t + m < tms)
        def _(m=m):
            for part in range(2):
                amp_copy(m, part).wait_send()
    for side in range(2):
        @pl.when(has[side])
        def _(side=side):
            for d in range(GHOST):
                co_copy(side, d).wait_send()

            def drain(i, _):
                plane_copy(i // STEPS, lax.rem(i, STEPS), side).wait_send()
                return 0

            lax.fori_loop(1, ROUNDS * STEPS, drain, 0)
    for copy in out_copies:
        copy.wait()


def solution(mesh):
    tms, spaces = mesh.shape["tm"], mesh.shape["space"]

    def shards(region_map, region_coef, source_cell, amplitude):
        cz, nx, ny = region_map.shape
        sources = source_cell.shape[0]
        planes = cz + 2 * GHOST + 2
        return pl.pallas_call(
            functools.partial(kernel, tms, spaces),
            out_shape=jax.ShapeDtypeStruct((1, 2, cz, nx, ny), jnp.float32),
            in_specs=[pl.BlockSpec(memory_space=pl.ANY)] * 4,
            out_specs=pl.BlockSpec(memory_space=pl.ANY),
            scratch_shapes=[
                pltpu.VMEM((cz, nx, ny), jnp.int32),
                pltpu.SMEM(region_coef.shape, jnp.float32),
                pltpu.VMEM((1, sources), jnp.int32),
                pltpu.VMEM((STEPS, sources), jnp.float32),
                pltpu.VMEM((2, planes, nx + 2 * ROW0, ny), jnp.float32),
                pltpu.VMEM((2, cz, nx + 2 * ROW0, ny), jnp.float32),
                pltpu.VMEM((planes, nx, ny), jnp.float32),
                pltpu.VMEM((ROUNDS, STEPS, 2, nx, ny), jnp.float32),
                pltpu.VMEM((ROUNDS, STEPS, 2, nx, ny), jnp.float32),
                pltpu.VMEM((2, cz, nx, ny), jnp.float32),
                pltpu.VMEM((cz // 2 * nx, sources), jnp.bfloat16),
                pltpu.VMEM((sources, 2 * ny), jnp.bfloat16),
                pltpu.VMEM((SPAN, STEPS, sources), jnp.float32),
                pltpu.VMEM((ROUNDS, PIECES, STEPS, sources), jnp.float32),
                pltpu.SemaphoreType.DMA((4,)),
                pltpu.SemaphoreType.DMA((2,)),
                pltpu.SemaphoreType.DMA((SPAN, 2)),
                pltpu.SemaphoreType.DMA((SPAN, 2)),
                pltpu.SemaphoreType.DMA((2, GHOST)),
                pltpu.SemaphoreType.DMA((2, GHOST)),
                pltpu.SemaphoreType.DMA((ROUNDS, STEPS, 2)),
                pltpu.SemaphoreType.DMA((ROUNDS, STEPS, 2)),
            ],
            compiler_params=pltpu.CompilerParams(
                collective_id=0, has_side_effects=True, vmem_limit_bytes=60 << 20
            ),
        )(region_map, region_coef, source_cell.reshape(1, sources), amplitude)

    placed = (P("space", None, None), P(), P("space"), P("tm", None, "space"))
    return jax.shard_map(
        shards, mesh=mesh, in_specs=placed, out_specs=P("tm", None, "space", None, None), check_vma=False
    )
```

time: 198 us -> 81 us (0.41)
  the two profiles are of different devices: /device:TPU:12 before, /device:TPU:78 now
where the time goes in v2:
time: 81 us; the launch traced here: 80.9 us
  Pallas kernels  78.5 us (97%)
  local copies, waits for them, and re-layouts  2.3 us (3%)
    pallas_call x1, Pallas kernels, shards(): pl.pallas_call(functools.partial(kernel, tms, spaces), out_shape=jax.Shap...  78.5 us
    unnamed x1, local copies, waits for them, and re-layouts  2.3 us

profile of v2, /device:TPU:78, one launch (start us, length us, event | category | flops | bytes accessed | tf_op | source)
XLA Modules:
  0.0 80.9 jit_solution(7042614642800689320)
XLA Ops:
  0.0 78.5 %shard_map.46 = f32[1,2,8,128,128]{4,3,2,1,0:T(8,128)} custom-call(s32[8,128,128]{2,1,0:T(8,128)} %region_in.1, f32[8]{0:T(128)} %coef_in.1, s32[1,1024]{1,0:T(1,128)} %bitcast.1, f32[1,8,1024]{2,1,0:T(8,128)} %amp_in.1), custom_call_target="tpu_custom_call" | custom-call | tf_op jit(solution)/shard_map/pallas_call | solution.py:350
  78.6 2.3 %copy.6 = f32[1,2,8,128,128]{4,3,2,1,0:T(8,128)} copy(f32[1,2,8,128,128]{4,3,2,1,0:T(8,128)} %shard_map.46) | data formatting | bytes 2097152

commit v3 on v2

--- a/solution.py
+++ b/solution.py
@@ -21,8 +21,8 @@
     tms, spaces,
     region_in, coef_in, cell_in, amp_in, out_ref,
     region_ref, coef_ref, cell_ref, amp_ref,
-    u, v, co, hist, send, force, rows_hot, cols_hot, amps, pieces,
-    local_sem, out_sem, amp_send, amp_recv, co_send, co_recv, plane_send, plane_recv,
+    u, v, co, hist, send, leak, first, through, force, rows_hot, cols_hot, amps, pieces,
+    local_sem, amp_send, amp_recv, co_send, co_recv, plane_send, plane_recv,
 ):
     t, s = lax.axis_index("tm"), lax.axis_index("space")
     cz, nx, ny = region_in.shape
@@ -115,6 +115,11 @@
             @pl.when(has[side])
             def _(side=side):
                 plane_wait(r, k, side).wait_recv()
+
+    through[...] = functools.reduce(jnp.multiply, [co[own + z] for z in range(cz)])
+
+    for side in range(2):
+        first[side] = zero_plane
 
     def clear_u(p, _):
         for i in range(2):
@@ -206,9 +211,8 @@
             base = base - field[later, p, inner, :]
         return base + speed * (around - 6.0 * c)
 
-    def run_alone(r, k):
+    def run_alone(r, k, planes):
         now, later = (k - 1) % 2, k % 2
-        depth = min(k, STEPS - k)
 
         def outside(z):
             return max(-z, z - cz + 1)
@@ -216,10 +220,13 @@
         def at(z):
             return u[now, own + z, inner, :] if outside(z) <= k - 1 else None
 
-        for z in range(-depth, cz + depth):
+        for z in planes:
             new = advance(u, now, later, own + z, co[own + z], at(z - 1), at(z + 1), outside(z) <= k - 1, outside(z) <= max(k - 2, 0))
             if 0 <= z < cz:
                 new = new + force[(k - 1) % 2, z]
+            elif k == STEPS:
+                leak[0 if z < 0 else 1] = new
+                continue
             u[later, own + z, inner, :] = new
             if k < STEPS and z == 0:
                 send[r, k, 0] = new
@@ -233,10 +240,9 @@
             return min(z + 1, cz - z)
 
         def at(z):
-            if z < 0:
-                return hist[r, k - 1, 0]
-            if z >= cz:
-                return hist[r, k - 1, 1]
+            if z < 0 or z >= cz:
+                side = 0 if z < 0 else 1
+                return hist[r, k - 1, side] if k > 1 else first[side]
             return v[now, z, inner, :] if inside(z) <= k - 1 else None
 
         for z in planes:
@@ -248,28 +254,23 @@
             if k >= STEPS - 1:
                 whole = u[later, own + z, inner, :] + new
                 u[later, own + z, inner, :] = whole
-                if k == STEPS and z in (0, cz - 1):
-                    send[lax.rem(r + 1, ROUNDS), 0, 0 if z == 0 else 1] = whole
+                out_ref[0, k - STEPS + 1, z] = whole
 
     for part in range(2):
         split_amplitude(SPAN, amp_ref[halves[part], :], part)
 
-    out_copies = [
-        pltpu.make_async_copy(u.at[1 - i, pl.ds(own, cz), inner, :], out_ref.at[0, i], out_sem.at[i]) for i in range(2)
-    ]
+    edges = (0, cz - 1)
 
     def one_round(r, _):
-        for m in range(1, SPAN):
-            @pl.when(r == SPAN - m)
-            def _(m=m):
-                for part in range(2):
-                    take_amplitude(m, part)
+        @pl.when(r > 0)
+        def _():
+            await_planes(r, 0)
+            for side in range(2):
+                first[side] = hist[r, 0, side] + leak[side]
 
         for k in range(1, STEPS + 1):
             @pl.when(r == 0)
             def _(k=k):
-                if k == 1:
-                    take_amplitude(SPAN, 0)
                 if k == FIRST + 1:
                     take_amplitude(SPAN, 1)
                 if k == STEPS // 2:
@@ -284,42 +285,54 @@
                         def _(side=side):
                             co_wait(side, k - 1).wait_recv()
 
-            make_force(r, k - 1)
-            run_alone(r, k)
-            if k < STEPS:
+            depth = min(k, STEPS + 1 - k)
+            if k > 1:
+                make_force(r, k - 1)
+            run_alone(r, k, [z for z in range(-depth, cz + depth) if k > 1 or z not in edges])
+            if 1 < k < STEPS:
                 send_planes(r, k)
+
+        following = lax.rem(r + 1, ROUNDS)
+        for side in range(2):
+            send[following, 0, side] = u[0, own + edges[side], inner, :] + through[...] * first[1 - side]
+
+        @pl.when(r < SPAN)
+        def _():
+            send_planes(r + 1, 0)
+
         for k in range(1, STEPS + 1):
-            if k == 1:
-                @pl.when(r > 0)
-                def _():
-                    await_planes(r, 0)
-                    run_caused(r, 1, range(cz))
-
-                @pl.when(r == 0)
-                def _():
-                    for z in (0, cz - 1):
-                        v[1, z, inner, :] = zero_plane
-            elif k < STEPS:
-                await_planes(r, k - 1)
-                run_caused(r, k, range(cz))
-                if k == STEPS - 1:
-                    @pl.when(r == SPAN)
-                    def _():
-                        out_copies[0].start()
-            else:
-                await_planes(r, k - 1)
-                run_caused(r, k, (0, cz - 1))
+            if k == STEPS:
+                for m in range(1, SPAN):
+                    @pl.when(r + 1 == SPAN - m)
+                    def _(m=m):
+                        for part in range(2):
+                            take_amplitude(m, part)
 
                 @pl.when(r < SPAN)
                 def _():
-                    send_planes(r + 1, 0)
-
-                run_caused(r, k, range(1, cz - 1))
+                    make_force(r + 1, 0)
+
+            if k > 1:
+                await_planes(r, k - 1)
+            if k < STEPS:
+                run_caused(r, k, range(cz))
+
+        run_caused(r, STEPS, (0, 1, cz - 2, cz - 1))
+
+        @pl.when(r < SPAN)
+        def _():
+            run_alone(r + 1, 1, edges)
+            send_planes(r + 1, 1)
+
+        run_caused(r, STEPS, range(2, cz - 2))
         return 0
 
+    take_amplitude(SPAN, 0)
+    make_force(0, 0)
+    run_alone(0, 1, edges)
+    send_planes(0, 1)
     lax.fori_loop(0, ROUNDS, one_round, 0)
 
-    out_copies[1].start()
     for m in range(1, SPAN + 1):
         @pl.when(t + m < tms)
         def _(m=m):
@@ -336,8 +349,6 @@
                 return 0
 
             lax.fori_loop(1, ROUNDS * STEPS, drain, 0)
-    for copy in out_copies:
-        copy.wait()
 
 
 def solution(mesh):
@@ -349,9 +360,9 @@
         planes = cz + 2 * GHOST + 2
         return pl.pallas_call(
             functools.partial(kernel, tms, spaces),
-            out_shape=jax.ShapeDtypeStruct((1, 2, cz, nx, ny), jnp.float32),
+            out_shape=pltpu.VMEM((1, 2, cz, nx, ny), jnp.float32),
             in_specs=[pl.BlockSpec(memory_space=pl.ANY)] * 4,
-            out_specs=pl.BlockSpec(memory_space=pl.ANY),
+            out_specs=pl.BlockSpec(memory_space=pltpu.VMEM),
             scratch_shapes=[
                 pltpu.VMEM((cz, nx, ny), jnp.int32),
                 pltpu.SMEM(region_coef.shape, jnp.float32),
@@ -362,13 +373,15 @@
                 pltpu.VMEM((planes, nx, ny), jnp.float32),
                 pltpu.VMEM((ROUNDS, STEPS, 2, nx, ny), jnp.float32),
                 pltpu.VMEM((ROUNDS, STEPS, 2, nx, ny), jnp.float32),
+                pltpu.VMEM((2, nx, ny), jnp.float32),
+                pltpu.VMEM((2, nx, ny), jnp.float32),
+                pltpu.VMEM((nx, ny), jnp.float32),
                 pltpu.VMEM((2, cz, nx, ny), jnp.float32),
                 pltpu.VMEM((cz // 2 * nx, sources), jnp.bfloat16),
                 pltpu.VMEM((sources, 2 * ny), jnp.bfloat16),
                 pltpu.VMEM((SPAN, STEPS, sources), jnp.float32),
                 pltpu.VMEM((ROUNDS, PIECES, STEPS, sources), jnp.float32),
                 pltpu.SemaphoreType.DMA((4,)),
-                pltpu.SemaphoreType.DMA((2,)),
                 pltpu.SemaphoreType.DMA((SPAN, 2)),
                 pltpu.SemaphoreType.DMA((SPAN, 2)),
                 pltpu.SemaphoreType.DMA((2, GHOST)),

time: 81 us -> 77.7 us (0.959)
  Pallas kernels: 78.5 us -> 76.6 us
  local copies, waits for them, and re-layouts: 2.3 us -> 0.97 us
    pallas_call x1, Pallas kernels: 78.5 us -> 76.6 us  [shards(): pl.pallas_call(functools.partial(kernel, tms, spaces), out_shape=pltpu.VM...]
    unnamed x1, local copies, waits for them, and re-layouts: 2.3 us -> 0.97 us
where the time goes in v3:
time: 77.7 us; the launch traced here: 77.6 us
  Pallas kernels  76.6 us (99%)
  local copies, waits for them, and re-layouts  0.97 us (1%)
    pallas_call x1, Pallas kernels, shards(): pl.pallas_call(functools.partial(kernel, tms, spaces), out_shape=pltpu.VM...  76.6 us

profile of v3, /device:TPU:78, one launch (start us, length us, event | category | flops | bytes accessed | tf_op | source)
XLA Modules:
  0.0 77.6 jit_solution(1300560645804488213)
XLA Ops:
  0.0 76.6 %shard_map.46 = f32[1,2,8,128,128]{4,3,2,1,0:T(8,128)S(1)} custom-call(s32[8,128,128]{2,1,0:T(8,128)} %region_in.1, f32[8]{0:T(128)} %coef_in.1, s32[1,1024]{1,0:T(1,128)} %bitcast.1, f32[1,8,1024]{2,1,0:T(8,128)} %amp_in.1), custom_call_target="tpu_custom_call" | custom-call | tf_op jit(solution)/shard_map/pallas_call | solution.py:361
  76.6 1.0 %copy.6 = f32[1,2,8,128,128]{4,3,2,1,0:T(8,128)} copy(f32[1,2,8,128,128]{4,3,2,1,0:T(8,128)S(1)} %shard_map.46) | data formatting | bytes 2097152

commit v4 on v3

--- a/solution.py
+++ b/solution.py
@@ -262,12 +262,6 @@
     edges = (0, cz - 1)
 
     def one_round(r, _):
-        @pl.when(r > 0)
-        def _():
-            await_planes(r, 0)
-            for side in range(2):
-                first[side] = hist[r, 0, side] + leak[side]
-
         for k in range(1, STEPS + 1):
             @pl.when(r == 0)
             def _(k=k):
@@ -285,6 +279,13 @@
                         def _(side=side):
                             co_wait(side, k - 1).wait_recv()
 
+            if k == STEPS - 2:
+                @pl.when(r > 0)
+                def _():
+                    await_planes(r, 0)
+                    for side in range(2):
+                        first[side] = hist[r, 0, side] + leak[side]
+
             depth = min(k, STEPS + 1 - k)
             if k > 1:
                 make_force(r, k - 1)
@@ -312,19 +313,20 @@
                 def _():
                     make_force(r + 1, 0)
 
+                run_caused(r, STEPS, range(1, cz - 1))
+
             if k > 1:
                 await_planes(r, k - 1)
             if k < STEPS:
                 run_caused(r, k, range(cz))
 
-        run_caused(r, STEPS, (0, 1, cz - 2, cz - 1))
+        run_caused(r, STEPS, edges)
 
         @pl.when(r < SPAN)
         def _():
             run_alone(r + 1, 1, edges)
             send_planes(r + 1, 1)
 
-        run_caused(r, STEPS, range(2, cz - 2))
         return 0
 
     take_amplitude(SPAN, 0)

time: 77.7 us -> 76.9 us (0.990)
  the two profiles are of different devices: /device:TPU:78 before, /device:TPU:121 now
where the time goes in v4:
time: 76.9 us; the launch traced here: 76.8 us
  Pallas kernels  75.8 us (99%)
  local copies, waits for them, and re-layouts  0.97 us (1%)
    pallas_call x1, Pallas kernels, shards(): pl.pallas_call(functools.partial(kernel, tms, spaces), out_shape=pltpu.VM...  75.8 us

profile of v4, /device:TPU:121, one launch (start us, length us, event | category | flops | bytes accessed | tf_op | source)
XLA Modules:
  0.0 76.8 jit_solution(10872346213283431299)
XLA Ops:
  0.0 75.8 %shard_map.46 = f32[1,2,8,128,128]{4,3,2,1,0:T(8,128)S(1)} custom-call(s32[8,128,128]{2,1,0:T(8,128)} %region_in.1, f32[8]{0:T(128)} %coef_in.1, s32[1,1024]{1,0:T(1,128)} %bitcast.1, f32[1,8,1024]{2,1,0:T(8,128)} %amp_in.1), custom_call_target="tpu_custom_call" | custom-call | tf_op jit(solution)/shard_map/pallas_call | solution.py:363
  75.8 1.0 %copy.6 = f32[1,2,8,128,128]{4,3,2,1,0:T(8,128)} copy(f32[1,2,8,128,128]{4,3,2,1,0:T(8,128)S(1)} %shard_map.46) | data formatting | bytes 2097152
